TPU v7x, 32 devices: a whole 2x2x4 slice. The times are simulated.
32 devices in a mesh: groups: 2 (over x), tile: 16 (over z, y, core).
Axes of the slice: x: 2, y: 2, z: 4, core: 2. Of those that a mesh axis runs over, the one named last changes fastest.
Arguments:
- fine_nodes: bfloat16 [32768, 512], P(('groups', 'tile')), parts along dimension 0, may hold values from -6 to 6
- fine_table: int32 [16384, 6], P('tile'), may hold values from 0 to 16383, as said below
- mid_table: int32 [4096, 6], P('tile'), may hold values from 0 to 4095, as said below
- coarse_table: int32 [1024, 6], replicated, may hold values from 0 to 1023, as said below
- fine_parent: int32 [16384], P('tile'), may hold values from 0 to 4095, as said below
- mid_parent: int32 [4096], P('tile'), may hold values from 0 to 1023, as said below
- edge_self: bfloat16 [3, 512, 512], replicated, may hold values from -0.1875 to 0.1875
- edge_peer: bfloat16 [3, 512, 512], replicated, may hold values from -0.1875 to 0.1875
- edge_bias: float32 [3, 512], replicated, may hold values from -3 to 3
- node_self: bfloat16 [3, 512, 512], replicated, may hold values from -0.1875 to 0.1875
- node_message: bfloat16 [3, 512, 512], replicated, may hold values from -0.109375 to 0.109375
- node_bias: float32 [3, 512], replicated, may hold values from -3 to 3
- node_out: bfloat16 [3, 512, 512], replicated, may hold values from -0.25 to 0.25
- ascend_gain: float32 [2, 512], replicated, may hold values from 0.1 to 1.9
- down_self: bfloat16 [2, 512, 512], replicated, may hold values from -0.1875 to 0.1875
- down_parent: bfloat16 [2, 512, 512], replicated, may hold values from -0.1875 to 0.1875
- down_bias: float32 [2, 512], replicated, may hold values from -3 to 3
- down_out: bfloat16 [2, 512, 512], replicated, may hold values from -0.25 to 0.25
Outputs:
- fine_out: bfloat16 [32768, 512], P(('groups', 'tile')), parts along dimension 0
- mid_out: bfloat16 [8192, 512], P(('groups', 'tile')), parts along dimension 0
- coarse_out: bfloat16 [2048, 512], P(('groups', 'tile')), parts along dimension 0
There are 2 independent parts, one for each index of `groups`. A program takes and returns all parts, laid end to end along the dimension named above; an argument that names none is the same for every part. Nothing has to cross between parts.
Inputs may be any that keep to these rules, and one draw needn't show every extreme that they name: `fine_table`: fine node n is grid cell (n // 256, n % 256); each of its six neighbours lies in its own grid row or one of the two rows beside it, columns wrapping around. `mid_table`: Level-1 node p is cell (p // 128, p % 128); each neighbour lies in its own row or one of the two rows beside it, columns wrapping around. `coarse_table`: any level-2 nodes. `fine_parent`: the parent of fine cell (r, c) lies in level-1 row r // 2 - 1, r // 2 or r // 2 + 1. `mid_parent`: the parent of level-1 cell (r, c) lies in level-2 row r // 2 - 1, r // 2 or r // 2 + 1.
All inputs are finite; a program needn't handle non-finite values.
Results may differ from a plain program's by a relative error of at most 0.014.
Values may be sent and summed in bfloat16 or wider, within the bound.
A program may use at most 64 MiB of HBM per device.

v0:
```python
import jax
import jax.numpy as jnp
from jax import lax
from jax.sharding import PartitionSpec as P

COLS = 256


def with_halo(cells, sides, width):
    for axis, dim in sides:
        count = lax.axis_size(axis)
        ends = count - 1
        head = lax.slice_in_dim(cells, 0, width, axis=dim)
        tail = lax.slice_in_dim(cells, cells.shape[dim] - width, cells.shape[dim], axis=dim)
        cells = jnp.concatenate(
            [
                lax.ppermute(tail, axis, [(i, (i + 1) % count) for i in range(ends)]),
                cells,
                lax.ppermute(head, axis, [((i + 1) % count, i) for i in range(ends)]),
            ],
            axis=dim,
        )
    return cells


def gelu_tanh(values):
    return jax.nn.gelu(values, approximate=True)


def rim_rows(block_rows, col_count):
    feature_count = block_rows.shape[1]
    grid_rows = block_rows.reshape(block_rows.shape[0] // col_count, col_count, feature_count)
    padded = with_halo(grid_rows, (("tile", 0),), 1)
    return padded.reshape(-1, feature_count)


def finish_level(node_rows, summed, level_index, weights):
    node_self = weights[3]
    node_message = weights[4]
    node_bias = weights[5]
    node_out = weights[6]
    message = summed.astype(jnp.bfloat16)
    pre_act = jnp.dot(node_rows, node_self[level_index], preferred_element_type=jnp.float32)
    pre_act = (
        pre_act
        + jnp.dot(message, node_message[level_index], preferred_element_type=jnp.float32)
        + node_bias[level_index]
    )
    hidden = gelu_tanh(pre_act).astype(jnp.bfloat16)
    result = node_rows.astype(jnp.float32) + jnp.dot(
        hidden, node_out[level_index], preferred_element_type=jnp.float32
    )
    return result.astype(jnp.bfloat16)


def own_projection(node_rows, level_index, weights):
    return (
        jnp.dot(node_rows, weights[0][level_index], preferred_element_type=jnp.float32)
        + weights[2][level_index]
    )


def peer_projection(node_rows, level_index, weights):
    return jnp.dot(node_rows, weights[1][level_index], preferred_element_type=jnp.float32).astype(
        jnp.bfloat16
    )


def process_local(node_rows, neighbours, level_index, col_count, weights):
    own_proj = own_projection(node_rows, level_index, weights)
    extended = rim_rows(peer_projection(node_rows, level_index, weights), col_count)
    offset = lax.axis_index("tile") * node_rows.shape[0] - col_count
    local_ids = neighbours - offset
    summed = jnp.zeros(own_proj.shape, jnp.float32)
    for slot_index in range(6):
        fetched = extended[local_ids[:, slot_index]].astype(jnp.float32)
        summed = summed + gelu_tanh(own_proj + fetched)
    return finish_level(node_rows, summed, level_index, weights)


def ascend_local(children, parents, col_up, gain_vec):
    feature_count = children.shape[1]
    rows_up = children.shape[0] // (4 * col_up)
    span_rows = (rows_up + 2) * col_up
    offset = lax.axis_index("tile") * rows_up * col_up - col_up
    local_ids = parents - offset
    onehot = (local_ids[None, :] == jnp.arange(span_rows, dtype=jnp.int32)[:, None]).astype(
        jnp.bfloat16
    )
    partial_value = jnp.dot(onehot, children, preferred_element_type=jnp.float32)
    grid_rows = partial_value.reshape(rows_up + 2, col_up, feature_count)
    padded = with_halo(grid_rows.astype(jnp.bfloat16), (("tile", 0),), 1).astype(grid_rows.dtype)
    summed = grid_rows[1:-1]
    summed = summed.at[0].add(padded[0])
    summed = summed.at[-1].add(padded[-1])
    summed = summed.reshape(rows_up * col_up, feature_count)
    scale_inv = lax.rsqrt(jnp.mean(summed * summed, axis=1, keepdims=True) + 1e-05)
    return (summed * scale_inv * gain_vec).astype(jnp.bfloat16)


def descend_local(children, lifted_ext, parents, col_up, level_index, downs):
    down_self, down_parent, down_bias, down_out = downs
    rows_up = children.shape[0] // (4 * col_up)
    offset = lax.axis_index("tile") * rows_up * col_up - col_up
    fetched = lifted_ext[parents - offset].astype(jnp.float32)
    pre_act = (
        jnp.dot(children, down_self[level_index], preferred_element_type=jnp.float32)
        + fetched
        + down_bias[level_index]
    )
    hidden = gelu_tanh(pre_act).astype(jnp.bfloat16)
    result = children.astype(jnp.float32) + jnp.dot(
        hidden, down_out[level_index], preferred_element_type=jnp.float32
    )
    return result.astype(jnp.bfloat16)


def local(
    fine_nodes,
    fine_table,
    mid_table,
    coarse_table,
    fine_parent,
    mid_parent,
    edge_self,
    edge_peer,
    edge_bias,
    node_self,
    node_message,
    node_bias,
    node_out,
    ascend_gain,
    down_self,
    down_parent,
    down_bias,
    down_out,
):
    weights = (edge_self, edge_peer, edge_bias, node_self, node_message, node_bias, node_out)
    downs = (down_self, down_parent, down_bias, down_out)
    col_mid = COLS // 2
    col_low = COLS // 4
    fine_rows = process_local(fine_nodes, fine_table, 0, COLS, weights)
    mid_start = ascend_local(fine_rows, fine_parent, col_mid, ascend_gain[0])
    mid_rows = process_local(mid_start, mid_table, 1, col_mid, weights)
    coarse_start = ascend_local(mid_rows, mid_parent, col_low, ascend_gain[1])
    coarse_count = coarse_start.shape[0]
    peer_proj = peer_projection(coarse_start, 2, weights)
    own_proj = own_projection(coarse_start, 2, weights)
    my_table = lax.dynamic_slice_in_dim(
        coarse_table, lax.axis_index("tile") * coarse_count, coarse_count, 0
    )
    running = jnp.zeros(own_proj.shape, jnp.float32)
    fragment = lax.all_gather(peer_proj, "tile", axis=0, tiled=True)
    row_count = fragment.shape[0]
    for slot_index in range(6):
        where_ids = my_table[:, slot_index]
        inside = (where_ids >= 0) & (where_ids < row_count)
        fetched = fragment[jnp.clip(where_ids, 0, row_count - 1)].astype(jnp.float32)
        running = running + jnp.where(inside[:, None], gelu_tanh(own_proj + fetched), 0.0)
    coarse_final = finish_level(coarse_start, running, 2, weights)
    lifted_own = jnp.dot(coarse_final, down_parent[1], preferred_element_type=jnp.float32).astype(
        jnp.bfloat16
    )
    lifted_ext = rim_rows(lifted_own, col_low)
    mid_final = descend_local(mid_rows, lifted_ext, mid_parent, col_low, 1, downs)
    lifted_mid = rim_rows(
        jnp.dot(mid_final, down_parent[0], preferred_element_type=jnp.float32).astype(jnp.bfloat16),
        col_mid,
    )
    fine_final = descend_local(fine_rows, lifted_mid, fine_parent, col_mid, 0, downs)
    return (fine_final, mid_final, coarse_final)


def solution(mesh):
    placed = (
        P(("groups", "tile"), None),
        P("tile", None),
        P("tile", None),
        P(),
        P("tile"),
        P("tile"),
        P(),
        P(),
        P(),
        P(),
        P(),
        P(),
        P(),
        P(),
        P(),
        P(),
        P(),
        P(),
    )
    return jax.shard_map(
        local,
        mesh=mesh,
        in_specs=placed,
        out_specs=(
            P(("groups", "tile"), None),
            P(("groups", "tile"), None),
            P(("groups", "tile"), None),
        ),
        check_vma=False,
    )
```

profile of v0, /device:TPU:5, one launch (start us, length us, event | category | flops | bytes accessed | tf_op | source)
XLA Modules:
  0.0 196.6 jit_solution(9857290049073583987)
XLA Ops:
  7.3 2.1 %convolution_convert_fusion = bf16[1024,512]{1,0:T(8,128)(2,1)S(1)} fusion(bf16[1024,512]{1,0:T(8,128)(2,1)} %param.26, bf16[3,512,512]{2,1,0:T(8,128)(2,1)} %param.33), kind=kOutput, calls=%fused_computation.97 | convolution fusion | flops 537395200 | bytes 2621440 | tf_op jit(solution)/shard_map/dot_general | solution.py:64
  9.5 3.8 %collective-permute-start = (bf16[1,256,512]{2,1,0:T(8,128)(2,1)S(1)}, bf16[1,256,512]{2,1,0:T(8,128)(2,1)S(1)}, u32[]{:S(2)}, u32[]{:S(2)}) collective-permute-start(bf16[1,256,512]{2,1,0:T(8,128)(2,1)S(1)} %get-tuple-element.57), channel_id=1, source_target_pairs={{0,1},{1,2},{2,3},{3,4},{4,5},{5,6},{6,7},{7,8},{8,9},{9,10},{10,1... | collective-permute-start | bytes 786440 | tf_op jit(solution)/shard_map/ppermute | solution.py:17
  13.4 1.9 collective-permute-start.1
  15.5 3.1 %fusion.175 = f32[1024,512]{1,0:T(8,128)} fusion(bf16[1024,512]{1,0:T(8,128)(2,1)S(1)} %copy-done.3, bf16[3,512,512]{2,1,0:T(8,128)(2,1)} %param.35), kind=kOutput, calls=%fused_computation.221 | convolution fusion | flops 536870912 | bytes 3670016 | tf_op jit(solution)/shard_map/dot_general | solution.py:43
  18.7 3.2 %collective-permute-done.1 = bf16[1,256,512]{2,1,0:T(8,128)(2,1)S(1)} collective-permute-done((bf16[1,256,512]{2,1,0:T(8,128)(2,1)S(1)}, bf16[1,256,512]{2,1,0:T(8,128)(2,1)S(1)}, u32[]{:S(2)}, u32[]{:S(2)}) %collective-permute-start.1) | collective-permute-done | bytes 262176 | tf_op jit(solution)/shard_map/ppermute | solution.py:19
  21.9 0.2 pad_maximum_fusion
  22.1 5.1 %gather_fusion = bf16[1024,512]{1,0:T(8,128)(2,1)} fusion(bf16[1536,512]{1,0:T(8,128)(2,1)S(1)} %bitcast.201, s32[1024]{0:T(1024)S(1)} %broadcast_clamp_fusion.5), kind=kCustom, calls=%fused_computation | custom fusion | bytes 2101248 | tf_op jit(solution)/shard_map/gather | solution.py:76
  27.2 5.1 %gather_fusion.1 = bf16[1024,512]{1,0:T(8,128)(2,1)} fusion(bf16[1536,512]{1,0:T(8,128)(2,1)S(1)} %bitcast.202, s32[1024]{0:T(1024)S(1)} %broadcast_clamp_fusion.4), kind=kCustom, calls=%fused_computation.1 | custom fusion | bytes 2101248 | tf_op jit(solution)/shard_map/gather | solution.py:76
  32.3 5.1 %gather_fusion.2 = bf16[1024,512]{1,0:T(8,128)(2,1)} fusion(bf16[1536,512]{1,0:T(8,128)(2,1)S(1)} %bitcast.203, s32[1024]{0:T(1024)S(1)} %broadcast_clamp_fusion.3), kind=kCustom, calls=%fused_computation.2 | custom fusion | bytes 2101248 | tf_op jit(solution)/shard_map/gather | solution.py:76
  37.4 5.0 %gather_fusion.3 = bf16[1024,512]{1,0:T(8,128)(2,1)} fusion(bf16[1536,512]{1,0:T(8,128)(2,1)S(1)} %bitcast.204, s32[1024]{0:T(1024)S(1)} %broadcast_clamp_fusion.2), kind=kCustom, calls=%fused_computation.3 | custom fusion | bytes 2101248 | tf_op jit(solution)/shard_map/gather | solution.py:76
  42.4 5.1 %gather_fusion.4 = bf16[1024,512]{1,0:T(8,128)(2,1)} fusion(bf16[1536,512]{1,0:T(8,128)(2,1)S(1)} %bitcast.205, s32[1024]{0:T(1024)S(1)} %broadcast_clamp_fusion.1), kind=kCustom, calls=%fused_computation.4 | custom fusion | bytes 2101248 | tf_op jit(solution)/shard_map/gather | solution.py:76
  47.5 5.1 %gather_fusion.5 = bf16[1024,512]{1,0:T(8,128)(2,1)} fusion(bf16[1536,512]{1,0:T(8,128)(2,1)S(1)} %bitcast.206, s32[1024]{0:T(1024)S(1)} %broadcast_clamp_fusion), kind=kCustom, calls=%fused_computation.5 | custom fusion | bytes 2101248 | tf_op jit(solution)/shard_map/gather | solution.py:76
  52.5 10.0 %fusion.54 = bf16[1024,512]{1,0:T(8,128)(2,1)S(1)} fusion(f32[1024,512]{1,0:T(8,128)} %fusion.175, f32[512]{0:T(512)S(1)} %bitcast.245, bf16[1024,512]{1,0:T(8,128)(2,1)} %gather_fusion.5, bf16[1024,512]{1,0:T(8,128)(2,1)} %gather_fusion.4, bf16[1024,512]{1,0:T(8,128)(2,1)} %gather_fusion.3, bf16[1024,512]{1,0:T(8,128)(2,1)} %gather_fusion.2, ...), kind=kOutput, calls=%fused_computation.82 | convolution fusion | flops 1114636288 | bytes 11538432 | tf_op jit(solution)/shard_map/dot_general | solution.py:46
  62.5 1.7 add_convert_fusion.1
  64.3 0.7 fusion.343
  65.1 1.9 collective-permute-start.2
  67.0 2.6 %collective-permute-start.3 = (bf16[1,128,512]{2,1,0:T(8,128)(2,1)S(1)}, bf16[1,128,512]{2,1,0:T(8,128)(2,1)S(1)}, u32[]{:S(2)}, u32[]{:S(2)}) collective-permute-start(bf16[1,128,512]{2,1,0:T(8,128)(2,1)S(1)} %get-tuple-element.60), channel_id=1, source_target_pairs={{1,0},{2,1},{3,2},{4,3},{5,4},{6,5},{7,6},{8,7},{9,8},{10,9},{11,1... | collective-permute-start | bytes 393224 | tf_op jit(solution)/shard_map/ppermute | solution.py:19
  69.7 4.5 %collective-permute-done.3 = bf16[1,128,512]{2,1,0:T(8,128)(2,1)S(1)} collective-permute-done((bf16[1,128,512]{2,1,0:T(8,128)(2,1)S(1)}, bf16[1,128,512]{2,1,0:T(8,128)(2,1)S(1)}, u32[]{:S(2)}, u32[]{:S(2)}) %collective-permute-start.3) | collective-permute-done | bytes 131104 | tf_op jit(solution)/shard_map/ppermute | solution.py:19
  74.3 0.1 multiply_reduce_fusion
  74.4 0.1 multiply_convert_fusion
  74.5 1.5 convolution_convert_fusion.2
  76.0 0.3 fusion.160
  76.4 1.9 collective-permute-start.4
  78.3 2.4 %collective-permute-start.5 = (bf16[1,128,512]{2,1,0:T(8,128)(2,1)S(1)}, bf16[1,128,512]{2,1,0:T(8,128)(2,1)S(1)}, u32[]{:S(2)}, u32[]{:S(2)}) collective-permute-start(bf16[1,128,512]{2,1,0:T(8,128)(2,1)S(1)} %get-tuple-element.64), channel_id=1, source_target_pairs={{1,0},{2,1},{3,2},{4,3},{5,4},{6,5},{7,6},{8,7},{9,8},{10,9},{11,1... | collective-permute-start | bytes 393224 | tf_op jit(solution)/shard_map/ppermute | solution.py:19
  80.7 1.3 convolution_add_fusion.3
  82.1 0.8 fusion.163
  82.9 2.6 %collective-permute-done.5 = bf16[1,128,512]{2,1,0:T(8,128)(2,1)S(1)} collective-permute-done((bf16[1,128,512]{2,1,0:T(8,128)(2,1)S(1)}, bf16[1,128,512]{2,1,0:T(8,128)(2,1)S(1)}, u32[]{:S(2)}, u32[]{:S(2)}) %collective-permute-start.5) | collective-permute-done | bytes 131104 | tf_op jit(solution)/shard_map/ppermute | solution.py:19
  85.5 1.2 gather_fusion.10
  86.7 1.9 gather_fusion.6
  88.6 1.9 gather_fusion.7
  90.4 1.9 gather_fusion.8
  92.3 1.9 gather_fusion.9
  94.2 1.9 gather_fusion.11
  96.0 3.3 %fusion.66 = bf16[256,512]{1,0:T(8,128)(2,1)S(1)} fusion(f32[256,512]{1,0:T(8,128)S(1)} %fusion.160, bf16[3,512,512]{2,1,0:T(8,128)(2,1)} %param.38, bf16[3,512,512]{2,1,0:T(8,128)(2,1)} %param.36, bf16[256,512]{1,0:T(8,128)(2,1)} %fusion.163, f32[256,512]{1,0:T(8,128)S(1)} %convolution_add_fusion.3, bf16[256,512]{1,0:T(8,128)(2,1)} %gather_fusion.11, ...), kind=kOutput, calls=%fused_computation.103 | convolution fusion | flops 278921216 | bytes 4196352 | tf_op jit(solution)/shard_map/dot_general | solution.py:50
  99.3 0.2 fusion.344
  99.5 1.9 collective-permute-start.6
  101.5 2.4 %collective-permute-start.7 = (bf16[1,64,512]{2,1,0:T(8,128)(2,1)S(1)}, bf16[1,64,512]{2,1,0:T(8,128)(2,1)S(1)}, u32[]{:S(2)}, u32[]{:S(2)}) collective-permute-start(bf16[1,64,512]{2,1,0:T(8,128)(2,1)S(1)} %get-tuple-element.66), channel_id=1, source_target_pairs={{1,0},{2,1},{3,2},{4,3},{5,4},{6,5},{7,6},{8,7},{9,8},{10,9},{11,1... | collective-permute-start | bytes 196616 | tf_op jit(solution)/shard_map/ppermute | solution.py:19
  103.9 4.1 %collective-permute-done.7 = bf16[1,64,512]{2,1,0:T(8,128)(2,1)S(1)} collective-permute-done((bf16[1,64,512]{2,1,0:T(8,128)(2,1)S(1)}, bf16[1,64,512]{2,1,0:T(8,128)(2,1)S(1)}, u32[]{:S(2)}, u32[]{:S(2)}) %collective-permute-start.7) | collective-permute-done | bytes 65568 | tf_op jit(solution)/shard_map/ppermute | solution.py:19
  107.9 0.1 multiply_reduce_fusion.1
  108.1 0.1 multiply_convert_fusion.1
  108.2 1.9 convolution_convert_fusion.4
  110.1 0.1 constant_dynamic-slice_fusion
  110.3 0.2 fusion.151
  110.5 36.7 %all-gather.2.cloned.1.call-done = bf16[1024,512]{1,0:T(8,128)(2,1)} async-done(((bf16[64,512]{1,0:T(8,128)(2,1)}), bf16[1024,512]{1,0:T(8,128)(2,1)}) %all-gather.2.cloned.1.call-update) | async-done | bytes 1048592 | tf_op jit(solution)/shard_map/all_gather | solution.py:153
  147.2 2.2 %gather_fusion.12 = bf16[64,512]{1,0:T(8,128)(2,1)S(1)} fusion(bf16[1024,512]{1,0:T(8,128)(2,1)} %all-gather.2.cloned.1.call-done, s32[1024]{0:T(1024)S(1)} %get-tuple-element.112), kind=kCustom, calls=%fused_computation.12 | custom fusion | bytes 131328 | tf_op jit(solution)/shard_map/gather | solution.py:158
  149.3 2.1 %gather_fusion.13 = bf16[64,512]{1,0:T(8,128)(2,1)S(1)} fusion(bf16[1024,512]{1,0:T(8,128)(2,1)} %all-gather.2.cloned.1.call-done, s32[1024]{0:T(1024)S(1)} %get-tuple-element.111), kind=kCustom, calls=%fused_computation.13 | custom fusion | bytes 131328 | tf_op jit(solution)/shard_map/gather | solution.py:158
  151.4 2.1 %gather_fusion.14 = bf16[64,512]{1,0:T(8,128)(2,1)S(1)} fusion(bf16[1024,512]{1,0:T(8,128)(2,1)} %all-gather.2.cloned.1.call-done, s32[1024]{0:T(1024)S(1)} %get-tuple-element.110), kind=kCustom, calls=%fused_computation.14 | custom fusion | bytes 131328 | tf_op jit(solution)/shard_map/gather | solution.py:158
  153.5 0.7 gather_fusion.15
  154.2 0.7 gather_fusion.16
  154.9 0.7 gather_fusion.17
  155.6 1.7 fusion.297
  157.3 1.6 fusion.69
  158.9 0.2 fusion.70
  159.1 3.4 %collective-permute-start.8 = (bf16[1,64,512]{2,1,0:T(8,128)(2,1)S(1)}, bf16[1,64,512]{2,1,0:T(8,128)(2,1)S(1)}, u32[]{:S(2)}, u32[]{:S(2)}) collective-permute-start(bf16[1,64,512]{2,1,0:T(8,128)(2,1)S(1)} %fusion.70), channel_id=1, source_target_pairs={{0,1},{1,2},{2,3},{3,4},{4,5},{5,6},{6,7},{7,8},{8,9},{9,10},{10,1... | collective-permute-start | bytes 196616 | tf_op jit(solution)/shard_map/ppermute | solution.py:17
  162.6 1.9 collective-permute-start.9
  164.5 4.5 %collective-permute-done.9 = bf16[1,64,512]{2,1,0:T(8,128)(2,1)S(1)} collective-permute-done((bf16[1,64,512]{2,1,0:T(8,128)(2,1)S(1)}, bf16[1,64,512]{2,1,0:T(8,128)(2,1)S(1)}, u32[]{:S(2)}, u32[]{:S(2)}) %collective-permute-start.9) | collective-permute-done | bytes 65568 | tf_op jit(solution)/shard_map/ppermute | solution.py:19
  169.1 1.2 gather_fusion.18
  170.2 1.7 fusion.67
  171.9 0.3 convolution_convert_fusion.1
  172.3 1.9 collective-permute-start.10
  174.2 2.4 %collective-permute-start.11 = (bf16[1,128,512]{2,1,0:T(8,128)(2,1)S(1)}, bf16[1,128,512]{2,1,0:T(8,128)(2,1)S(1)}, u32[]{:S(2)}, u32[]{:S(2)}) collective-permute-start(bf16[1,128,512]{2,1,0:T(8,128)(2,1)S(1)} %get-tuple-element.62), channel_id=1, source_target_pairs={{1,0},{2,1},{3,2},{4,3},{5,4},{6,5},{7,6},{8,7},{9,8},{10,9},{11,1... | collective-permute-start | bytes 393224 | tf_op jit(solution)/shard_map/ppermute | solution.py:19
  176.6 4.8 %collective-permute-done.11 = bf16[1,128,512]{2,1,0:T(8,128)(2,1)S(1)} collective-permute-done((bf16[1,128,512]{2,1,0:T(8,128)(2,1)S(1)}, bf16[1,128,512]{2,1,0:T(8,128)(2,1)S(1)}, u32[]{:S(2)}, u32[]{:S(2)}) %collective-permute-start.11) | collective-permute-done | bytes 131104 | tf_op jit(solution)/shard_map/ppermute | solution.py:19
  181.4 4.0 %gather_fusion.19 = bf16[1024,512]{1,0:T(8,128)(2,1)S(1)} fusion(bf16[512,512]{1,0:T(8,128)(2,1)S(1)} %bitcast.213, s32[1024]{0:T(1024)S(1)} %get-tuple-element.51), kind=kCustom, calls=%fused_computation.19 | custom fusion | bytes 2101248 | tf_op jit(solution)/shard_map/gather | solution.py:105
  185.4 4.3 %add_convert_fusion = bf16[1024,512]{1,0:T(8,128)(2,1)} fusion(bf16[1024,512]{1,0:T(8,128)(2,1)} %copy-done.17, bf16[1024,512]{1,0:T(8,128)(2,1)S(1)} %gather_fusion.19, f32[512]{0:T(512)S(1)} %bitcast.244, bf16[2,512,512]{2,1,0:T(8,128)(2,1)S(1)} %copy-done.15, bf16[2,512,512]{2,1,0:T(8,128)(2,1)} %param.40), kind=kOutput, calls=%fused_computation.91 | convolution fusion | flops 1081606144 | bytes 5244928 | tf_op jit(solution)/shard_map/dot_general | solution.py:112
  (85 shorter events, 0.8 us)
Async XLA Ops:
  7.2 102.9 %copy-start = (s32[1024,6]{0,1:T(8,128)S(1)}, s32[1024,6]{0,1:T(8,128)}, u32[]{:S(2)}) copy-start(s32[1024,6]{0,1:T(8,128)} %param.29) | copy-start | bytes 73732
  7.2 8.3 %copy-start.3 = (bf16[1024,512]{1,0:T(8,128)(2,1)S(1)}, bf16[1024,512]{1,0:T(8,128)(2,1)}, u32[]{:S(2)}) copy-start(bf16[1024,512]{1,0:T(8,128)(2,1)} %param.26) | copy-start | bytes 3145732
  7.2 8.1 %copy-start.7 = (s32[1024,6]{0,1:T(8,128)S(1)}, s32[1024,6]{0,1:T(8,128)}, u32[]{:S(2)}) copy-start(s32[1024,6]{0,1:T(8,128)} %param.27) | copy-start | bytes 73732
  7.2 8.2 %copy-start.9 = (f32[3,512]{1,0:T(4,128)S(1)}, f32[3,512]{1,0:T(4,128)}, u32[]{:S(2)}) copy-start(f32[3,512]{1,0:T(4,128)} %param.37) | copy-start | bytes 18436
  7.2 139.9 %all-gather.2.cloned.1.call-start = ((), (), s32[]{:S(2)}) async-start(), calls=%async_computation | async-start | bytes 1114112 | tf_op jit(solution)/shard_map/all_gather | solution.py:153
  9.4 9.1 %copy-start.12 = (f32[2,512]{1,0:T(2,128)S(1)}, f32[2,512]{1,0:T(2,128)}, u32[]{:S(2)}) copy-start(f32[2,512]{1,0:T(2,128)} %param.39) | copy-start | bytes 12292
  9.5 9.1 %copy-start.11 = (s32[1024]{0:T(1024)S(1)}, s32[1024]{0:T(1024)}, u32[]{:S(2)}) copy-start(s32[1024]{0:T(1024)} %param.30) | copy-start | bytes 12292
  9.5 9.1 %copy-start.8 = (s32[256,6]{0,1:T(8,128)S(1)}, s32[256,6]{0,1:T(8,128)}, u32[]{:S(2)}) copy-start(s32[256,6]{0,1:T(8,128)} %param.28) | copy-start | bytes 18436
  9.5 9.2 %copy-start.14 = (s32[256]{0:T(256)S(1)}, s32[256]{0:T(256)}, u32[]{:S(2)}) copy-start(s32[256]{0:T(256)} %param.31) | copy-start | bytes 3076
  9.5 9.2 %copy-start.10 = (f32[3,512]{1,0:T(4,128)S(1)}, f32[3,512]{1,0:T(4,128)}, u32[]{:S(2)}) copy-start(f32[3,512]{1,0:T(4,128)} %param.34) | copy-start | bytes 18436
  9.5 9.2 %collective-permute-start = (bf16[1,256,512]{2,1,0:T(8,128)(2,1)S(1)}, bf16[1,256,512]{2,1,0:T(8,128)(2,1)S(1)}, u32[]{:S(2)}, u32[]{:S(2)}) collective-permute-start(bf16[1,256,512]{2,1,0:T(8,128)(2,1)S(1)} %get-tuple-element.57), channel_id=1, source_target_pairs={{0,1},{1,2},{2,3},{3,4},{4,5},{5,6},{6,7},{7,8},{8,9},{9,10},{10,1... | collective-permute-start | bytes 786440 | tf_op jit(solution)/shard_map/ppermute | solution.py:17
  13.4 8.6 %collective-permute-start.1 = (bf16[1,256,512]{2,1,0:T(8,128)(2,1)S(1)}, bf16[1,256,512]{2,1,0:T(8,128)(2,1)S(1)}, u32[]{:S(2)}, u32[]{:S(2)}) collective-permute-start(bf16[1,256,512]{2,1,0:T(8,128)(2,1)S(1)} %get-tuple-element.58), channel_id=1, source_target_pairs={{1,0},{2,1},{3,2},{4,3},{5,4},{6,5},{7,6},{8,7},{9,8},{10,9},{11,1... | collective-permute-start | bytes 786440 | tf_op jit(solution)/shard_map/ppermute | solution.py:19
  47.5 5.1 %copy-start.4 = (bf16[1024,512]{1,0:T(8,128)(2,1)S(1)}, bf16[1024,512]{1,0:T(8,128)(2,1)}, u32[]{:S(2)}) copy-start(bf16[1024,512]{1,0:T(8,128)(2,1)} %param.26) | copy-start | bytes 3145732
  64.3 5.4 %copy-start.17 = (bf16[1024,512]{1,0:T(8,128)(2,1)}, bf16[1024,512]{1,0:T(8,128)(2,1)S(1)}, u32[]{:S(2)}) copy-start(bf16[1024,512]{1,0:T(8,128)(2,1)S(1)} %add_convert_fusion.1) | copy-start | bytes 3145732
  65.1 4.6 %collective-permute-start.2 = (bf16[1,128,512]{2,1,0:T(8,128)(2,1)S(1)}, bf16[1,128,512]{2,1,0:T(8,128)(2,1)S(1)}, u32[]{:S(2)}, u32[]{:S(2)}) collective-permute-start(bf16[1,128,512]{2,1,0:T(8,128)(2,1)S(1)} %get-tuple-element.59), channel_id=1, source_target_pairs={{0,1},{1,2},{2,3},{3,4},{4,5},{5,6},{6,7},{7,8},{8,9},{9,10},{10,1... | collective-permute-start | bytes 393224 | tf_op jit(solution)/shard_map/ppermute | solution.py:17
  67.0 7.2 %collective-permute-start.3 = (bf16[1,128,512]{2,1,0:T(8,128)(2,1)S(1)}, bf16[1,128,512]{2,1,0:T(8,128)(2,1)S(1)}, u32[]{:S(2)}, u32[]{:S(2)}) collective-permute-start(bf16[1,128,512]{2,1,0:T(8,128)(2,1)S(1)} %get-tuple-element.60), channel_id=1, source_target_pairs={{1,0},{2,1},{3,2},{4,3},{5,4},{6,5},{7,6},{8,7},{9,8},{10,9},{11,1... | collective-permute-start | bytes 393224 | tf_op jit(solution)/shard_map/ppermute | solution.py:19
  74.2 1.8 copy-start.2
  76.4 6.5 %collective-permute-start.4 = (bf16[1,128,512]{2,1,0:T(8,128)(2,1)S(1)}, bf16[1,128,512]{2,1,0:T(8,128)(2,1)S(1)}, u32[]{:S(2)}, u32[]{:S(2)}) collective-permute-start(bf16[1,128,512]{2,1,0:T(8,128)(2,1)S(1)} %get-tuple-element.63), channel_id=1, source_target_pairs={{0,1},{1,2},{2,3},{3,4},{4,5},{5,6},{6,7},{7,8},{8,9},{9,10},{10,1... | collective-permute-start | bytes 393224 | tf_op jit(solution)/shard_map/ppermute | solution.py:17
  78.3 7.2 %collective-permute-start.5 = (bf16[1,128,512]{2,1,0:T(8,128)(2,1)S(1)}, bf16[1,128,512]{2,1,0:T(8,128)(2,1)S(1)}, u32[]{:S(2)}, u32[]{:S(2)}) collective-permute-start(bf16[1,128,512]{2,1,0:T(8,128)(2,1)S(1)} %get-tuple-element.64), channel_id=1, source_target_pairs={{1,0},{2,1},{3,2},{4,3},{5,4},{6,5},{7,6},{8,7},{9,8},{10,9},{11,1... | collective-permute-start | bytes 393224 | tf_op jit(solution)/shard_map/ppermute | solution.py:19
  99.3 11.0 %copy-start.13 = (f32[2,512]{1,0:T(2,128)S(1)}, f32[2,512]{1,0:T(2,128)}, u32[]{:S(2)}) copy-start(f32[2,512]{1,0:T(2,128)} %param.42) | copy-start | bytes 12292
  99.5 4.3 %collective-permute-start.6 = (bf16[1,64,512]{2,1,0:T(8,128)(2,1)S(1)}, bf16[1,64,512]{2,1,0:T(8,128)(2,1)S(1)}, u32[]{:S(2)}, u32[]{:S(2)}) collective-permute-start(bf16[1,64,512]{2,1,0:T(8,128)(2,1)S(1)} %get-tuple-element.65), channel_id=1, source_target_pairs={{0,1},{1,2},{2,3},{3,4},{4,5},{5,6},{6,7},{7,8},{8,9},{9,10},{10,1... | collective-permute-start | bytes 196616 | tf_op jit(solution)/shard_map/ppermute | solution.py:17
  101.5 6.5 %collective-permute-start.7 = (bf16[1,64,512]{2,1,0:T(8,128)(2,1)S(1)}, bf16[1,64,512]{2,1,0:T(8,128)(2,1)S(1)}, u32[]{:S(2)}, u32[]{:S(2)}) collective-permute-start(bf16[1,64,512]{2,1,0:T(8,128)(2,1)S(1)} %get-tuple-element.66), channel_id=1, source_target_pairs={{1,0},{2,1},{3,2},{4,3},{5,4},{6,5},{7,6},{8,7},{9,8},{10,9},{11,1... | collective-permute-start | bytes 196616 | tf_op jit(solution)/shard_map/ppermute | solution.py:19
  147.2 6.3 %copy-start.1 = (bf16[1024,512]{1,0:T(8,128)(2,1)S(1)}, bf16[1024,512]{1,0:T(8,128)(2,1)}, u32[]{:S(2)}) copy-start(bf16[1024,512]{1,0:T(8,128)(2,1)} %all-gather.2.cloned.1.call-done) | copy-start | bytes 3145732
  155.6 3.3 %copy-start.5 = (bf16[2,512,512]{2,1,0:T(8,128)(2,1)S(1)}, bf16[2,512,512]{2,1,0:T(8,128)(2,1)}, u32[]{:S(2)}) copy-start(bf16[2,512,512]{2,1,0:T(8,128)(2,1)} %param.41) | copy-start | bytes 3145732
  158.9 13.0 %copy-start.6 = (bf16[64,512]{1,0:T(8,128)(2,1)}, bf16[64,512]{1,0:T(8,128)(2,1)S(1)}, u32[]{:S(2)}) copy-start(bf16[64,512]{1,0:T(8,128)(2,1)S(1)} %fusion.69) | copy-start | bytes 196612
  158.9 11.3 %copy-start.15 = (bf16[2,512,512]{2,1,0:T(8,128)(2,1)S(1)}, bf16[2,512,512]{2,1,0:T(8,128)(2,1)}, u32[]{:S(2)}) copy-start(bf16[2,512,512]{2,1,0:T(8,128)(2,1)} %param.43) | copy-start | bytes 3145732
  159.1 5.4 %collective-permute-start.8 = (bf16[1,64,512]{2,1,0:T(8,128)(2,1)S(1)}, bf16[1,64,512]{2,1,0:T(8,128)(2,1)S(1)}, u32[]{:S(2)}, u32[]{:S(2)}) collective-permute-start(bf16[1,64,512]{2,1,0:T(8,128)(2,1)S(1)} %fusion.70), channel_id=1, source_target_pairs={{0,1},{1,2},{2,3},{3,4},{4,5},{5,6},{6,7},{7,8},{8,9},{9,10},{10,1... | collective-permute-start | bytes 196616 | tf_op jit(solution)/shard_map/ppermute | solution.py:17
  162.6 6.5 %collective-permute-start.9 = (bf16[1,64,512]{2,1,0:T(8,128)(2,1)S(1)}, bf16[1,64,512]{2,1,0:T(8,128)(2,1)S(1)}, u32[]{:S(2)}, u32[]{:S(2)}) collective-permute-start(bf16[1,64,512]{2,1,0:T(8,128)(2,1)S(1)} %fusion.70), channel_id=1, source_target_pairs={{1,0},{2,1},{3,2},{4,3},{5,4},{6,5},{7,6},{8,7},{9,8},{10,9},{11,1... | collective-permute-start | bytes 196616 | tf_op jit(solution)/shard_map/ppermute | solution.py:19
  171.9 13.5 %copy-start.16 = (bf16[256,512]{1,0:T(8,128)(2,1)}, bf16[256,512]{1,0:T(8,128)(2,1)S(1)}, u32[]{:S(2)}) copy-start(bf16[256,512]{1,0:T(8,128)(2,1)S(1)} %fusion.67) | copy-start | bytes 786436
  172.3 4.3 %collective-permute-start.10 = (bf16[1,128,512]{2,1,0:T(8,128)(2,1)S(1)}, bf16[1,128,512]{2,1,0:T(8,128)(2,1)S(1)}, u32[]{:S(2)}, u32[]{:S(2)}) collective-permute-start(bf16[1,128,512]{2,1,0:T(8,128)(2,1)S(1)} %get-tuple-element.61), channel_id=1, source_target_pairs={{0,1},{1,2},{2,3},{3,4},{4,5},{5,6},{6,7},{7,8},{8,9},{9,10},{10,1... | collective-permute-start | bytes 393224 | tf_op jit(solution)/shard_map/ppermute | solution.py:17
  174.2 7.2 %collective-permute-start.11 = (bf16[1,128,512]{2,1,0:T(8,128)(2,1)S(1)}, bf16[1,128,512]{2,1,0:T(8,128)(2,1)S(1)}, u32[]{:S(2)}, u32[]{:S(2)}) collective-permute-start(bf16[1,128,512]{2,1,0:T(8,128)(2,1)S(1)} %get-tuple-element.62), channel_id=1, source_target_pairs={{1,0},{2,1},{3,2},{4,3},{5,4},{6,5},{7,6},{8,7},{9,8},{10,9},{11,1... | collective-permute-start | bytes 393224 | tf_op jit(solution)/shard_map/ppermute | solution.py:19
Sparse Core Ops, SparseCore 0:
  110.2 36.9 all-gather.1
where the time goes:
time: 198 us; the launch traced here: 197 us
  waiting for transfers between devices  60.4 us (31%)
  local copies, waits for them, and re-layouts  54.7 us (28%)
  matrix products  36.1 us (18%)
  starting transfers between devices  28.6 us (14%)
  between operations  14.9 us (8%)
    gather x12, local copies, waits for them, and re-layouts, process_local(): fetched = extended[local_ids[:, slot_index]].astype(jnp.float32)  40.9 us
    all_gather x1, waiting for transfers between devices, local(): fragment = lax.all_gather(peer_proj, 'tile', axis=0, tiled=True)  36.7 us
    ppermute x6, waiting for transfers between devices, with_halo(): lax.ppermute(head, axis, [((i + 1) % count, i) for i in range(ends)])  23.7 us
    ppermute x6, starting transfers between devices, with_halo(): lax.ppermute(tail, axis, [(i, (i + 1) % count) for i in range(ends)])  14.9 us
    ppermute x6, starting transfers between devices, with_halo(): lax.ppermute(head, axis, [((i + 1) % count, i) for i in range(ends)])  13.6 us
    dot_general x1, matrix products, finish_level(): jnp.dot(message, node_message[level_index], preferred_element_type=jnp.fl...  9.98 us
    gather x6, local copies, waits for them, and re-layouts, local(): fragment[jnp.clip(where_ids, 0, row_count - 1)].astype(jnp.float32)  8.41 us
    dot_general x3, matrix products, finish_level(): jnp.dot(hidden, node_out[level_index], preferred_element_type=jnp.float32)  6.61 us
  transfers between devices with their start and end apart: 13, of which 7 were waited for; matrix products, arithmetic and copies ran while one was open for 3% of the time, Pallas kernels for 0%

commit v1 on v0

--- a/solution.py
+++ b/solution.py
@@ -150,7 +150,9 @@
         coarse_table, lax.axis_index("tile") * coarse_count, coarse_count, 0
     )
     running = jnp.zeros(own_proj.shape, jnp.float32)
-    fragment = lax.all_gather(peer_proj, "tile", axis=0, tiled=True)
+    fragment = jnp.concatenate(
+        lax.all_to_all(jnp.stack([peer_proj] * lax.axis_size("tile")), "tile", 0, 0), axis=0
+    )
     row_count = fragment.shape[0]
     for slot_index in range(6):
         where_ids = my_table[:, slot_index]

time: 198 us -> 173 us (0.87)
  waiting for transfers between devices: 60.4 us -> 46.8 us
  between operations: 14.9 us -> 1.49 us
  starting transfers between devices: 28.6 us -> 34.3 us
  local copies, waits for them, and re-layouts: 54.7 us -> 51.6 us
    all_gather x1 -> x0, waiting for transfers between devices: 36.7 us -> none  [local(): fragment = lax.all_gather(peer_proj, 'tile', axis=0, tiled=True)]
    all_to_all x0 -> x1, waiting for transfers between devices: none -> 23.1 us  [local(): lax.all_to_all(jnp.stack([peer_proj] * lax.axis_size('tile')), 'tile', 0, 0)]
    all_to_all x0 -> x1, starting transfers between devices: none -> 5.06 us  [local(): lax.all_to_all(jnp.stack([peer_proj] * lax.axis_size('tile')), 'tile', 0, 0)]
    gather x6, local copies, waits for them, and re-layouts: 8.41 us -> 4.21 us  [local(): fragment[jnp.clip(where_ids, 0, row_count - 1)].astype(jnp.float32)]
where the time goes in v1:
time: 173 us; the launch traced here: 172 us
  local copies, waits for them, and re-layouts  51.6 us (30%)
  waiting for transfers between devices  46.8 us (27%)
  matrix products  35.5 us (21%)
  starting transfers between devices  34.3 us (20%)
  other arithmetic  1.88 us (1%)
    gather x12, local copies, waits for them, and re-layouts, process_local(): fetched = extended[local_ids[:, slot_index]].astype(jnp.float32)  40.9 us
    ppermute x6, waiting for transfers between devices, with_halo(): lax.ppermute(head, axis, [((i + 1) % count, i) for i in range(ends)])  23.7 us
    all_to_all x1, waiting for transfers between devices, local(): lax.all_to_all(jnp.stack([peer_proj] * lax.axis_size('tile')), 'tile', 0, 0)  23.1 us
    ppermute x6, starting transfers between devices, with_halo(): lax.ppermute(tail, axis, [(i, (i + 1) % count) for i in range(ends)])  15.6 us
    ppermute x6, starting transfers between devices, with_halo(): lax.ppermute(head, axis, [((i + 1) % count, i) for i in range(ends)])  13.6 us
    dot_general x1, matrix products, finish_level(): jnp.dot(message, node_message[level_index], preferred_element_type=jnp.fl...  9.98 us
    dot_general x3, matrix products, finish_level(): jnp.dot(hidden, node_out[level_index], preferred_element_type=jnp.float32)  6.61 us
    dot_general x2, matrix products, descend_local(): jnp.dot(hidden, down_out[level_index], preferred_element_type=jnp.float32)  6.04 us
  transfers between devices with their start and end apart: 13, of which 7 were waited for; matrix products, arithmetic and copies ran while one was open for 3% of the time, Pallas kernels for 0%

profile of v1, /device:TPU:5, one launch (start us, length us, event | category | flops | bytes accessed | tf_op | source)
XLA Modules:
  0.0 171.6 jit_solution(11951607838813817216)
XLA Ops:
  0.7 2.1 %convolution_convert_fusion = bf16[1024,512]{1,0:T(8,128)(2,1)S(1)} fusion(bf16[1024,512]{1,0:T(8,128)(2,1)} %param.26, bf16[3,512,512]{2,1,0:T(8,128)(2,1)} %param.33), kind=kOutput, calls=%fused_computation.97 | convolution fusion | flops 537395200 | bytes 2621440 | tf_op jit(solution)/shard_map/dot_general | solution.py:64
  2.9 3.8 %collective-permute-start = (bf16[1,256,512]{2,1,0:T(8,128)(2,1)S(1)}, bf16[1,256,512]{2,1,0:T(8,128)(2,1)S(1)}, u32[]{:S(2)}, u32[]{:S(2)}) collective-permute-start(bf16[1,256,512]{2,1,0:T(8,128)(2,1)S(1)} %get-tuple-element.57), channel_id=1, source_target_pairs={{0,1},{1,2},{2,3},{3,4},{4,5},{5,6},{6,7},{7,8},{8,9},{9,10},{10,1... | collective-permute-start | bytes 786440 | tf_op jit(solution)/shard_map/ppermute | solution.py:17
  6.8 1.9 %collective-permute-start.1 = (bf16[1,256,512]{2,1,0:T(8,128)(2,1)S(1)}, bf16[1,256,512]{2,1,0:T(8,128)(2,1)S(1)}, u32[]{:S(2)}, u32[]{:S(2)}) collective-permute-start(bf16[1,256,512]{2,1,0:T(8,128)(2,1)S(1)} %get-tuple-element.58), channel_id=1, source_target_pairs={{1,0},{2,1},{3,2},{4,3},{5,4},{6,5},{7,6},{8,7},{9,8},{10,9},{11,1... | collective-permute-start | bytes 786440 | tf_op jit(solution)/shard_map/ppermute | solution.py:19
  8.9 3.1 %fusion.175 = f32[1024,512]{1,0:T(8,128)} fusion(bf16[1024,512]{1,0:T(8,128)(2,1)S(1)} %copy-done.2, bf16[3,512,512]{2,1,0:T(8,128)(2,1)} %param.35), kind=kOutput, calls=%fused_computation.221 | convolution fusion | flops 536870912 | bytes 3670016 | tf_op jit(solution)/shard_map/dot_general | solution.py:43
  12.2 3.2 %collective-permute-done.1 = bf16[1,256,512]{2,1,0:T(8,128)(2,1)S(1)} collective-permute-done((bf16[1,256,512]{2,1,0:T(8,128)(2,1)S(1)}, bf16[1,256,512]{2,1,0:T(8,128)(2,1)S(1)}, u32[]{:S(2)}, u32[]{:S(2)}) %collective-permute-start.1) | collective-permute-done | bytes 262176 | tf_op jit(solution)/shard_map/ppermute | solution.py:19
  15.4 0.2 pad_maximum_fusion
  15.6 5.1 %gather_fusion = bf16[1024,512]{1,0:T(8,128)(2,1)} fusion(bf16[1536,512]{1,0:T(8,128)(2,1)S(1)} %bitcast.202, s32[1024]{0:T(1024)S(1)} %broadcast_clamp_fusion.5), kind=kCustom, calls=%fused_computation | custom fusion | bytes 2101248 | tf_op jit(solution)/shard_map/gather | solution.py:76
  20.6 5.1 %gather_fusion.1 = bf16[1024,512]{1,0:T(8,128)(2,1)} fusion(bf16[1536,512]{1,0:T(8,128)(2,1)S(1)} %bitcast.203, s32[1024]{0:T(1024)S(1)} %broadcast_clamp_fusion.4), kind=kCustom, calls=%fused_computation.1 | custom fusion | bytes 2101248 | tf_op jit(solution)/shard_map/gather | solution.py:76
  25.7 5.1 %gather_fusion.2 = bf16[1024,512]{1,0:T(8,128)(2,1)} fusion(bf16[1536,512]{1,0:T(8,128)(2,1)S(1)} %bitcast.204, s32[1024]{0:T(1024)S(1)} %broadcast_clamp_fusion.3), kind=kCustom, calls=%fused_computation.2 | custom fusion | bytes 2101248 | tf_op jit(solution)/shard_map/gather | solution.py:76
  30.8 5.0 %gather_fusion.3 = bf16[1024,512]{1,0:T(8,128)(2,1)} fusion(bf16[1536,512]{1,0:T(8,128)(2,1)S(1)} %bitcast.205, s32[1024]{0:T(1024)S(1)} %broadcast_clamp_fusion.2), kind=kCustom, calls=%fused_computation.3 | custom fusion | bytes 2101248 | tf_op jit(solution)/shard_map/gather | solution.py:76
  35.8 5.1 %gather_fusion.4 = bf16[1024,512]{1,0:T(8,128)(2,1)} fusion(bf16[1536,512]{1,0:T(8,128)(2,1)S(1)} %bitcast.206, s32[1024]{0:T(1024)S(1)} %broadcast_clamp_fusion.1), kind=kCustom, calls=%fused_computation.4 | custom fusion | bytes 2101248 | tf_op jit(solution)/shard_map/gather | solution.py:76
  40.9 5.1 %gather_fusion.5 = bf16[1024,512]{1,0:T(8,128)(2,1)} fusion(bf16[1536,512]{1,0:T(8,128)(2,1)S(1)} %bitcast.207, s32[1024]{0:T(1024)S(1)} %broadcast_clamp_fusion), kind=kCustom, calls=%fused_computation.5 | custom fusion | bytes 2101248 | tf_op jit(solution)/shard_map/gather | solution.py:76
  46.0 10.0 %fusion.54 = bf16[1024,512]{1,0:T(8,128)(2,1)S(1)} fusion(f32[1024,512]{1,0:T(8,128)} %fusion.175, f32[512]{0:T(512)S(1)} %bitcast.253, bf16[1024,512]{1,0:T(8,128)(2,1)} %gather_fusion.5, bf16[1024,512]{1,0:T(8,128)(2,1)} %gather_fusion.4, bf16[1024,512]{1,0:T(8,128)(2,1)} %gather_fusion.3, bf16[1024,512]{1,0:T(8,128)(2,1)} %gather_fusion.2, ...), kind=kOutput, calls=%fused_computation.82 | convolution fusion | flops 1114636288 | bytes 11538432 | tf_op jit(solution)/shard_map/dot_general | solution.py:46
  56.0 1.7 %add_convert_fusion.1 = bf16[1024,512]{1,0:T(8,128)(2,1)S(1)} fusion(bf16[1024,512]{1,0:T(8,128)(2,1)S(1)} %copy-done.3, bf16[1024,512]{1,0:T(8,128)(2,1)S(1)} %fusion.54, bf16[3,512,512]{2,1,0:T(8,128)(2,1)} %param.38), kind=kOutput, calls=%fused_computation.93 | convolution fusion | flops 538443776 | bytes 3670016 | tf_op jit(solution)/shard_map/dot_general | solution.py:50
  57.7 0.7 fusion.343
  58.5 1.9 %collective-permute-start.2 = (bf16[1,128,512]{2,1,0:T(8,128)(2,1)S(1)}, bf16[1,128,512]{2,1,0:T(8,128)(2,1)S(1)}, u32[]{:S(2)}, u32[]{:S(2)}) collective-permute-start(bf16[1,128,512]{2,1,0:T(8,128)(2,1)S(1)} %get-tuple-element.59), channel_id=1, source_target_pairs={{0,1},{1,2},{2,3},{3,4},{4,5},{5,6},{6,7},{7,8},{8,9},{9,10},{10,1... | collective-permute-start | bytes 393224 | tf_op jit(solution)/shard_map/ppermute | solution.py:17
  60.4 2.6 %collective-permute-start.3 = (bf16[1,128,512]{2,1,0:T(8,128)(2,1)S(1)}, bf16[1,128,512]{2,1,0:T(8,128)(2,1)S(1)}, u32[]{:S(2)}, u32[]{:S(2)}) collective-permute-start(bf16[1,128,512]{2,1,0:T(8,128)(2,1)S(1)} %get-tuple-element.60), channel_id=1, source_target_pairs={{1,0},{2,1},{3,2},{4,3},{5,4},{6,5},{7,6},{8,7},{9,8},{10,9},{11,1... | collective-permute-start | bytes 393224 | tf_op jit(solution)/shard_map/ppermute | solution.py:19
  63.1 4.5 %collective-permute-done.3 = bf16[1,128,512]{2,1,0:T(8,128)(2,1)S(1)} collective-permute-done((bf16[1,128,512]{2,1,0:T(8,128)(2,1)S(1)}, bf16[1,128,512]{2,1,0:T(8,128)(2,1)S(1)}, u32[]{:S(2)}, u32[]{:S(2)}) %collective-permute-start.3) | collective-permute-done | bytes 131104 | tf_op jit(solution)/shard_map/ppermute | solution.py:19
  67.7 0.1 multiply_reduce_fusion
  67.8 0.1 multiply_convert_fusion
  68.0 1.5 convolution_convert_fusion.2
  69.5 0.3 fusion.160
  69.8 1.9 %collective-permute-start.4 = (bf16[1,128,512]{2,1,0:T(8,128)(2,1)S(1)}, bf16[1,128,512]{2,1,0:T(8,128)(2,1)S(1)}, u32[]{:S(2)}, u32[]{:S(2)}) collective-permute-start(bf16[1,128,512]{2,1,0:T(8,128)(2,1)S(1)} %get-tuple-element.63), channel_id=1, source_target_pairs={{0,1},{1,2},{2,3},{3,4},{4,5},{5,6},{6,7},{7,8},{8,9},{9,10},{10,1... | collective-permute-start | bytes 393224 | tf_op jit(solution)/shard_map/ppermute | solution.py:17
  71.7 2.4 %collective-permute-start.5 = (bf16[1,128,512]{2,1,0:T(8,128)(2,1)S(1)}, bf16[1,128,512]{2,1,0:T(8,128)(2,1)S(1)}, u32[]{:S(2)}, u32[]{:S(2)}) collective-permute-start(bf16[1,128,512]{2,1,0:T(8,128)(2,1)S(1)} %get-tuple-element.64), channel_id=1, source_target_pairs={{1,0},{2,1},{3,2},{4,3},{5,4},{6,5},{7,6},{8,7},{9,8},{10,9},{11,1... | collective-permute-start | bytes 393224 | tf_op jit(solution)/shard_map/ppermute | solution.py:19
  74.1 1.3 convolution_add_fusion.3
  75.5 0.8 fusion.163
  76.3 2.6 %collective-permute-done.5 = bf16[1,128,512]{2,1,0:T(8,128)(2,1)S(1)} collective-permute-done((bf16[1,128,512]{2,1,0:T(8,128)(2,1)S(1)}, bf16[1,128,512]{2,1,0:T(8,128)(2,1)S(1)}, u32[]{:S(2)}, u32[]{:S(2)}) %collective-permute-start.5) | collective-permute-done | bytes 131104 | tf_op jit(solution)/shard_map/ppermute | solution.py:19
  79.0 1.2 gather_fusion.10
  80.1 1.9 %gather_fusion.6 = bf16[256,512]{1,0:T(8,128)(2,1)} fusion(bf16[512,512]{1,0:T(8,128)(2,1)S(1)} %bitcast.209, s32[1024]{0:T(1024)S(1)} %pad_clamp_fusion.12), kind=kCustom, calls=%fused_computation.6 | custom fusion | bytes 525312 | tf_op jit(solution)/shard_map/gather | solution.py:76
  82.0 1.9 %gather_fusion.7 = bf16[256,512]{1,0:T(8,128)(2,1)} fusion(bf16[512,512]{1,0:T(8,128)(2,1)S(1)} %bitcast.210, s32[1024]{0:T(1024)S(1)} %pad_clamp_fusion.11), kind=kCustom, calls=%fused_computation.7 | custom fusion | bytes 525312 | tf_op jit(solution)/shard_map/gather | solution.py:76
  83.8 1.9 %gather_fusion.8 = bf16[256,512]{1,0:T(8,128)(2,1)} fusion(bf16[512,512]{1,0:T(8,128)(2,1)S(1)} %bitcast.211, s32[1024]{0:T(1024)S(1)} %pad_clamp_fusion.10), kind=kCustom, calls=%fused_computation.8 | custom fusion | bytes 525312 | tf_op jit(solution)/shard_map/gather | solution.py:76
  85.7 1.9 %gather_fusion.9 = bf16[256,512]{1,0:T(8,128)(2,1)} fusion(bf16[512,512]{1,0:T(8,128)(2,1)S(1)} %bitcast.212, s32[1024]{0:T(1024)S(1)} %pad_clamp_fusion.9), kind=kCustom, calls=%fused_computation.9 | custom fusion | bytes 525312 | tf_op jit(solution)/shard_map/gather | solution.py:76
  87.6 1.9 %gather_fusion.11 = bf16[256,512]{1,0:T(8,128)(2,1)} fusion(bf16[512,512]{1,0:T(8,128)(2,1)S(1)} %bitcast.213, s32[1024]{0:T(1024)S(1)} %pad_clamp_fusion.7), kind=kCustom, calls=%fused_computation.11 | custom fusion | bytes 525312 | tf_op jit(solution)/shard_map/gather | solution.py:76
  89.4 3.3 %fusion.66 = bf16[256,512]{1,0:T(8,128)(2,1)S(1)} fusion(f32[256,512]{1,0:T(8,128)S(1)} %fusion.160, bf16[3,512,512]{2,1,0:T(8,128)(2,1)} %param.38, bf16[3,512,512]{2,1,0:T(8,128)(2,1)} %param.36, bf16[256,512]{1,0:T(8,128)(2,1)} %fusion.163, f32[256,512]{1,0:T(8,128)S(1)} %convolution_add_fusion.3, bf16[256,512]{1,0:T(8,128)(2,1)} %gather_fusion.11, ...), kind=kOutput, calls=%fused_computation.103 | convolution fusion | flops 278921216 | bytes 4196352 | tf_op jit(solution)/shard_map/dot_general | solution.py:50
  92.7 0.2 fusion.344
  93.0 1.9 %collective-permute-start.6 = (bf16[1,64,512]{2,1,0:T(8,128)(2,1)S(1)}, bf16[1,64,512]{2,1,0:T(8,128)(2,1)S(1)}, u32[]{:S(2)}, u32[]{:S(2)}) collective-permute-start(bf16[1,64,512]{2,1,0:T(8,128)(2,1)S(1)} %get-tuple-element.65), channel_id=1, source_target_pairs={{0,1},{1,2},{2,3},{3,4},{4,5},{5,6},{6,7},{7,8},{8,9},{9,10},{10,1... | collective-permute-start | bytes 196616 | tf_op jit(solution)/shard_map/ppermute | solution.py:17
  94.9 2.4 %collective-permute-start.7 = (bf16[1,64,512]{2,1,0:T(8,128)(2,1)S(1)}, bf16[1,64,512]{2,1,0:T(8,128)(2,1)S(1)}, u32[]{:S(2)}, u32[]{:S(2)}) collective-permute-start(bf16[1,64,512]{2,1,0:T(8,128)(2,1)S(1)} %get-tuple-element.66), channel_id=1, source_target_pairs={{1,0},{2,1},{3,2},{4,3},{5,4},{6,5},{7,6},{8,7},{9,8},{10,9},{11,1... | collective-permute-start | bytes 196616 | tf_op jit(solution)/shard_map/ppermute | solution.py:19
  97.3 4.1 %collective-permute-done.7 = bf16[1,64,512]{2,1,0:T(8,128)(2,1)S(1)} collective-permute-done((bf16[1,64,512]{2,1,0:T(8,128)(2,1)S(1)}, bf16[1,64,512]{2,1,0:T(8,128)(2,1)S(1)}, u32[]{:S(2)}, u32[]{:S(2)}) %collective-permute-start.7) | collective-permute-done | bytes 65568 | tf_op jit(solution)/shard_map/ppermute | solution.py:19
  101.4 0.1 multiply_reduce_fusion.1
  101.6 1.2 convolution_convert_fusion.4
  102.9 1.1 stack.2
  103.9 5.1 %all-to-all-start = ((bf16[16,64,512]{2,1,0:T(8,128)(2,1)}), bf16[16,64,512]{2,1,0:T(8,128)(2,1)S(1)}, u32[]{:S(2)}, u32[]{:S(2)}) async-start(bf16[16,64,512]{2,1,0:T(8,128)(2,1)} %stack.2), calls=%async_computation | async-start | bytes 2097152 | tf_op jit(solution)/shard_map/all_to_all | solution.py:154
  109.2 0.2 fusion.151
  109.4 23.1 %all-to-all-done = bf16[16,64,512]{2,1,0:T(8,128)(2,1)S(1)} async-done(((bf16[16,64,512]{2,1,0:T(8,128)(2,1)}), bf16[16,64,512]{2,1,0:T(8,128)(2,1)S(1)}, u32[]{:S(2)}, u32[]{:S(2)}) %all-to-all-start) | async-done | bytes 1048608 | tf_op jit(solution)/shard_map/all_to_all | solution.py:154
  132.5 0.7 gather_fusion.12
  133.2 0.7 gather_fusion.13
  133.9 0.7 gather_fusion.14
  134.6 0.7 gather_fusion.15
  135.3 0.7 gather_fusion.16
  136.0 0.7 gather_fusion.17
  136.7 1.7 fusion.297
  138.4 1.6 fusion.69
  140.1 0.2 fusion.70
  140.3 4.1 %collective-permute-start.8 = (bf16[1,64,512]{2,1,0:T(8,128)(2,1)S(1)}, bf16[1,64,512]{2,1,0:T(8,128)(2,1)S(1)}, u32[]{:S(2)}, u32[]{:S(2)}) collective-permute-start(bf16[1,64,512]{2,1,0:T(8,128)(2,1)S(1)} %fusion.70), channel_id=1, source_target_pairs={{0,1},{1,2},{2,3},{3,4},{4,5},{5,6},{6,7},{7,8},{8,9},{9,10},{10,1... | collective-permute-start | bytes 196616 | tf_op jit(solution)/shard_map/ppermute | solution.py:17
  144.3 1.9 %collective-permute-start.9 = (bf16[1,64,512]{2,1,0:T(8,128)(2,1)S(1)}, bf16[1,64,512]{2,1,0:T(8,128)(2,1)S(1)}, u32[]{:S(2)}, u32[]{:S(2)}) collective-permute-start(bf16[1,64,512]{2,1,0:T(8,128)(2,1)S(1)} %fusion.70), channel_id=1, source_target_pairs={{1,0},{2,1},{3,2},{4,3},{5,4},{6,5},{7,6},{8,7},{9,8},{10,9},{11,1... | collective-permute-start | bytes 196616 | tf_op jit(solution)/shard_map/ppermute | solution.py:19
  146.3 4.5 %collective-permute-done.9 = bf16[1,64,512]{2,1,0:T(8,128)(2,1)S(1)} collective-permute-done((bf16[1,64,512]{2,1,0:T(8,128)(2,1)S(1)}, bf16[1,64,512]{2,1,0:T(8,128)(2,1)S(1)}, u32[]{:S(2)}, u32[]{:S(2)}) %collective-permute-start.9) | collective-permute-done | bytes 65568 | tf_op jit(solution)/shard_map/ppermute | solution.py:19
  150.9 1.2 gather_fusion.18
  152.0 1.7 fusion.67
  153.7 0.3 convolution_convert_fusion.1
  154.1 1.9 %collective-permute-start.10 = (bf16[1,128,512]{2,1,0:T(8,128)(2,1)S(1)}, bf16[1,128,512]{2,1,0:T(8,128)(2,1)S(1)}, u32[]{:S(2)}, u32[]{:S(2)}) collective-permute-start(bf16[1,128,512]{2,1,0:T(8,128)(2,1)S(1)} %get-tuple-element.61), channel_id=1, source_target_pairs={{0,1},{1,2},{2,3},{3,4},{4,5},{5,6},{6,7},{7,8},{8,9},{9,10},{10,1... | collective-permute-start | bytes 393224 | tf_op jit(solution)/shard_map/ppermute | solution.py:17
  156.0 2.4 %collective-permute-start.11 = (bf16[1,128,512]{2,1,0:T(8,128)(2,1)S(1)}, bf16[1,128,512]{2,1,0:T(8,128)(2,1)S(1)}, u32[]{:S(2)}, u32[]{:S(2)}) collective-permute-start(bf16[1,128,512]{2,1,0:T(8,128)(2,1)S(1)} %get-tuple-element.62), channel_id=1, source_target_pairs={{1,0},{2,1},{3,2},{4,3},{5,4},{6,5},{7,6},{8,7},{9,8},{10,9},{11,1... | collective-permute-start | bytes 393224 | tf_op jit(solution)/shard_map/ppermute | solution.py:19
  158.4 4.8 %collective-permute-done.11 = bf16[1,128,512]{2,1,0:T(8,128)(2,1)S(1)} collective-permute-done((bf16[1,128,512]{2,1,0:T(8,128)(2,1)S(1)}, bf16[1,128,512]{2,1,0:T(8,128)(2,1)S(1)}, u32[]{:S(2)}, u32[]{:S(2)}) %collective-permute-start.11) | collective-permute-done | bytes 131104 | tf_op jit(solution)/shard_map/ppermute | solution.py:19
  163.2 4.0 %gather_fusion.19 = bf16[1024,512]{1,0:T(8,128)(2,1)S(1)} fusion(bf16[512,512]{1,0:T(8,128)(2,1)S(1)} %bitcast.214, s32[1024]{0:T(1024)S(1)} %get-tuple-element.51), kind=kCustom, calls=%fused_computation.19 | custom fusion | bytes 2101248 | tf_op jit(solution)/shard_map/gather | solution.py:105
  167.2 4.4 %add_convert_fusion = bf16[1024,512]{1,0:T(8,128)(2,1)} fusion(bf16[1024,512]{1,0:T(8,128)(2,1)} %copy-done.18, bf16[1024,512]{1,0:T(8,128)(2,1)S(1)} %gather_fusion.19, f32[512]{0:T(512)S(1)} %bitcast.251, bf16[2,512,512]{2,1,0:T(8,128)(2,1)S(1)} %copy-done.16, bf16[2,512,512]{2,1,0:T(8,128)(2,1)} %param.40), kind=kOutput, calls=%fused_computation.91 | convolution fusion | flops 1081606144 | bytes 5244928 | tf_op jit(solution)/shard_map/dot_general | solution.py:112
  (87 shorter events, 0.9 us)
Async XLA Ops:
  0.6 108.4 %copy-start = (s32[1024,6]{0,1:T(8,128)S(1)}, s32[1024,6]{0,1:T(8,128)}, u32[]{:S(2)}) copy-start(s32[1024,6]{0,1:T(8,128)} %param.29) | copy-start | bytes 73732
  0.6 8.2 %copy-start.2 = (bf16[1024,512]{1,0:T(8,128)(2,1)S(1)}, bf16[1024,512]{1,0:T(8,128)(2,1)}, u32[]{:S(2)}) copy-start(bf16[1024,512]{1,0:T(8,128)(2,1)} %param.26) | copy-start | bytes 3145732
  0.7 8.1 %copy-start.8 = (s32[1024,6]{0,1:T(8,128)S(1)}, s32[1024,6]{0,1:T(8,128)}, u32[]{:S(2)}) copy-start(s32[1024,6]{0,1:T(8,128)} %param.27) | copy-start | bytes 73732
  0.7 8.2 %copy-start.10 = (f32[3,512]{1,0:T(4,128)S(1)}, f32[3,512]{1,0:T(4,128)}, u32[]{:S(2)}) copy-start(f32[3,512]{1,0:T(4,128)} %param.37) | copy-start | bytes 18436
  2.9 9.1 %copy-start.13 = (f32[2,512]{1,0:T(2,128)S(1)}, f32[2,512]{1,0:T(2,128)}, u32[]{:S(2)}) copy-start(f32[2,512]{1,0:T(2,128)} %param.39) | copy-start | bytes 12292
  2.9 9.1 %copy-start.12 = (s32[1024]{0:T(1024)S(1)}, s32[1024]{0:T(1024)}, u32[]{:S(2)}) copy-start(s32[1024]{0:T(1024)} %param.30) | copy-start | bytes 12292
  2.9 9.1 %copy-start.9 = (s32[256,6]{0,1:T(8,128)S(1)}, s32[256,6]{0,1:T(8,128)}, u32[]{:S(2)}) copy-start(s32[256,6]{0,1:T(8,128)} %param.28) | copy-start | bytes 18436
  2.9 9.2 %copy-start.15 = (s32[256]{0:T(256)S(1)}, s32[256]{0:T(256)}, u32[]{:S(2)}) copy-start(s32[256]{0:T(256)} %param.31) | copy-start | bytes 3076
  2.9 9.2 %copy-start.11 = (f32[3,512]{1,0:T(4,128)S(1)}, f32[3,512]{1,0:T(4,128)}, u32[]{:S(2)}) copy-start(f32[3,512]{1,0:T(4,128)} %param.34) | copy-start | bytes 18436
  2.9 9.2 %collective-permute-start = (bf16[1,256,512]{2,1,0:T(8,128)(2,1)S(1)}, bf16[1,256,512]{2,1,0:T(8,128)(2,1)S(1)}, u32[]{:S(2)}, u32[]{:S(2)}) collective-permute-start(bf16[1,256,512]{2,1,0:T(8,128)(2,1)S(1)} %get-tuple-element.57), channel_id=1, source_target_pairs={{0,1},{1,2},{2,3},{3,4},{4,5},{5,6},{6,7},{7,8},{8,9},{9,10},{10,1... | collective-permute-start | bytes 786440 | tf_op jit(solution)/shard_map/ppermute | solution.py:17
  6.8 8.6 %collective-permute-start.1 = (bf16[1,256,512]{2,1,0:T(8,128)(2,1)S(1)}, bf16[1,256,512]{2,1,0:T(8,128)(2,1)S(1)}, u32[]{:S(2)}, u32[]{:S(2)}) collective-permute-start(bf16[1,256,512]{2,1,0:T(8,128)(2,1)S(1)} %get-tuple-element.58), channel_id=1, source_target_pairs={{1,0},{2,1},{3,2},{4,3},{5,4},{6,5},{7,6},{8,7},{9,8},{10,9},{11,1... | collective-permute-start | bytes 786440 | tf_op jit(solution)/shard_map/ppermute | solution.py:19
  40.9 5.1 %copy-start.3 = (bf16[1024,512]{1,0:T(8,128)(2,1)S(1)}, bf16[1024,512]{1,0:T(8,128)(2,1)}, u32[]{:S(2)}) copy-start(bf16[1024,512]{1,0:T(8,128)(2,1)} %param.26) | copy-start | bytes 3145732
  57.7 5.4 %copy-start.18 = (bf16[1024,512]{1,0:T(8,128)(2,1)}, bf16[1024,512]{1,0:T(8,128)(2,1)S(1)}, u32[]{:S(2)}) copy-start(bf16[1024,512]{1,0:T(8,128)(2,1)S(1)} %add_convert_fusion.1) | copy-start | bytes 3145732
  58.5 4.6 %collective-permute-start.2 = (bf16[1,128,512]{2,1,0:T(8,128)(2,1)S(1)}, bf16[1,128,512]{2,1,0:T(8,128)(2,1)S(1)}, u32[]{:S(2)}, u32[]{:S(2)}) collective-permute-start(bf16[1,128,512]{2,1,0:T(8,128)(2,1)S(1)} %get-tuple-element.59), channel_id=1, source_target_pairs={{0,1},{1,2},{2,3},{3,4},{4,5},{5,6},{6,7},{7,8},{8,9},{9,10},{10,1... | collective-permute-start | bytes 393224 | tf_op jit(solution)/shard_map/ppermute | solution.py:17
  60.4 7.2 %collective-permute-start.3 = (bf16[1,128,512]{2,1,0:T(8,128)(2,1)S(1)}, bf16[1,128,512]{2,1,0:T(8,128)(2,1)S(1)}, u32[]{:S(2)}, u32[]{:S(2)}) collective-permute-start(bf16[1,128,512]{2,1,0:T(8,128)(2,1)S(1)} %get-tuple-element.60), channel_id=1, source_target_pairs={{1,0},{2,1},{3,2},{4,3},{5,4},{6,5},{7,6},{8,7},{9,8},{10,9},{11,1... | collective-permute-start | bytes 393224 | tf_op jit(solution)/shard_map/ppermute | solution.py:19
  67.6 1.8 %copy-start.1 = (bf16[3,512,512]{2,1,0:T(8,128)(2,1)S(1)}, bf16[3,512,512]{2,1,0:T(8,128)(2,1)}, u32[]{:S(2)}) copy-start(bf16[3,512,512]{2,1,0:T(8,128)(2,1)} %param.35) | copy-start | bytes 4718596
  69.8 6.5 %collective-permute-start.4 = (bf16[1,128,512]{2,1,0:T(8,128)(2,1)S(1)}, bf16[1,128,512]{2,1,0:T(8,128)(2,1)S(1)}, u32[]{:S(2)}, u32[]{:S(2)}) collective-permute-start(bf16[1,128,512]{2,1,0:T(8,128)(2,1)S(1)} %get-tuple-element.63), channel_id=1, source_target_pairs={{0,1},{1,2},{2,3},{3,4},{4,5},{5,6},{6,7},{7,8},{8,9},{9,10},{10,1... | collective-permute-start | bytes 393224 | tf_op jit(solution)/shard_map/ppermute | solution.py:17
  71.7 7.2 %collective-permute-start.5 = (bf16[1,128,512]{2,1,0:T(8,128)(2,1)S(1)}, bf16[1,128,512]{2,1,0:T(8,128)(2,1)S(1)}, u32[]{:S(2)}, u32[]{:S(2)}) collective-permute-start(bf16[1,128,512]{2,1,0:T(8,128)(2,1)S(1)} %get-tuple-element.64), channel_id=1, source_target_pairs={{1,0},{2,1},{3,2},{4,3},{5,4},{6,5},{7,6},{8,7},{9,8},{10,9},{11,1... | collective-permute-start | bytes 393224 | tf_op jit(solution)/shard_map/ppermute | solution.py:19
  92.7 8.7 %copy-start.5 = (bf16[256,512]{1,0:T(8,128)(2,1)}, bf16[256,512]{1,0:T(8,128)(2,1)S(1)}, u32[]{:S(2)}) copy-start(bf16[256,512]{1,0:T(8,128)(2,1)S(1)} %fusion.66) | copy-start | bytes 786436
  93.0 4.3 %collective-permute-start.6 = (bf16[1,64,512]{2,1,0:T(8,128)(2,1)S(1)}, bf16[1,64,512]{2,1,0:T(8,128)(2,1)S(1)}, u32[]{:S(2)}, u32[]{:S(2)}) collective-permute-start(bf16[1,64,512]{2,1,0:T(8,128)(2,1)S(1)} %get-tuple-element.65), channel_id=1, source_target_pairs={{0,1},{1,2},{2,3},{3,4},{4,5},{5,6},{6,7},{7,8},{8,9},{9,10},{10,1... | collective-permute-start | bytes 196616 | tf_op jit(solution)/shard_map/ppermute | solution.py:17
  94.9 6.5 %collective-permute-start.7 = (bf16[1,64,512]{2,1,0:T(8,128)(2,1)S(1)}, bf16[1,64,512]{2,1,0:T(8,128)(2,1)S(1)}, u32[]{:S(2)}, u32[]{:S(2)}) collective-permute-start(bf16[1,64,512]{2,1,0:T(8,128)(2,1)S(1)} %get-tuple-element.66), channel_id=1, source_target_pairs={{1,0},{2,1},{3,2},{4,3},{5,4},{6,5},{7,6},{8,7},{9,8},{10,9},{11,1... | collective-permute-start | bytes 196616 | tf_op jit(solution)/shard_map/ppermute | solution.py:19
  101.5 7.7 %copy-start.14 = (f32[2,512]{1,0:T(2,128)S(1)}, f32[2,512]{1,0:T(2,128)}, u32[]{:S(2)}) copy-start(f32[2,512]{1,0:T(2,128)} %param.42) | copy-start | bytes 12292
  103.9 28.6 %all-to-all-start = ((bf16[16,64,512]{2,1,0:T(8,128)(2,1)}), bf16[16,64,512]{2,1,0:T(8,128)(2,1)S(1)}, u32[]{:S(2)}, u32[]{:S(2)}) async-start(bf16[16,64,512]{2,1,0:T(8,128)(2,1)} %stack.2), calls=%async_computation | async-start | bytes 2097152 | tf_op jit(solution)/shard_map/all_to_all | solution.py:154
  136.7 3.3 %copy-start.4 = (bf16[2,512,512]{2,1,0:T(8,128)(2,1)S(1)}, bf16[2,512,512]{2,1,0:T(8,128)(2,1)}, u32[]{:S(2)}) copy-start(bf16[2,512,512]{2,1,0:T(8,128)(2,1)} %param.41) | copy-start | bytes 3145732
  140.0 13.7 %copy-start.7 = (bf16[64,512]{1,0:T(8,128)(2,1)}, bf16[64,512]{1,0:T(8,128)(2,1)S(1)}, u32[]{:S(2)}) copy-start(bf16[64,512]{1,0:T(8,128)(2,1)S(1)} %fusion.69) | copy-start | bytes 196612
  140.0 12.0 %copy-start.6 = (bf16[256,512]{1,0:T(8,128)(2,1)S(1)}, bf16[256,512]{1,0:T(8,128)(2,1)}, u32[]{:S(2)}) copy-start(bf16[256,512]{1,0:T(8,128)(2,1)} %copy-done.5) | copy-start | bytes 786436
  140.1 12.0 %copy-start.16 = (bf16[2,512,512]{2,1,0:T(8,128)(2,1)S(1)}, bf16[2,512,512]{2,1,0:T(8,128)(2,1)}, u32[]{:S(2)}) copy-start(bf16[2,512,512]{2,1,0:T(8,128)(2,1)} %param.43) | copy-start | bytes 3145732
  140.3 6.0 %collective-permute-start.8 = (bf16[1,64,512]{2,1,0:T(8,128)(2,1)S(1)}, bf16[1,64,512]{2,1,0:T(8,128)(2,1)S(1)}, u32[]{:S(2)}, u32[]{:S(2)}) collective-permute-start(bf16[1,64,512]{2,1,0:T(8,128)(2,1)S(1)} %fusion.70), channel_id=1, source_target_pairs={{0,1},{1,2},{2,3},{3,4},{4,5},{5,6},{6,7},{7,8},{8,9},{9,10},{10,1... | collective-permute-start | bytes 196616 | tf_op jit(solution)/shard_map/ppermute | solution.py:17
  144.3 6.5 %collective-permute-start.9 = (bf16[1,64,512]{2,1,0:T(8,128)(2,1)S(1)}, bf16[1,64,512]{2,1,0:T(8,128)(2,1)S(1)}, u32[]{:S(2)}, u32[]{:S(2)}) collective-permute-start(bf16[1,64,512]{2,1,0:T(8,128)(2,1)S(1)} %fusion.70), channel_id=1, source_target_pairs={{1,0},{2,1},{3,2},{4,3},{5,4},{6,5},{7,6},{8,7},{9,8},{10,9},{11,1... | collective-permute-start | bytes 196616 | tf_op jit(solution)/shard_map/ppermute | solution.py:19
  153.7 13.5 %copy-start.17 = (bf16[256,512]{1,0:T(8,128)(2,1)}, bf16[256,512]{1,0:T(8,128)(2,1)S(1)}, u32[]{:S(2)}) copy-start(bf16[256,512]{1,0:T(8,128)(2,1)S(1)} %fusion.67) | copy-start | bytes 786436
  154.1 4.3 %collective-permute-start.10 = (bf16[1,128,512]{2,1,0:T(8,128)(2,1)S(1)}, bf16[1,128,512]{2,1,0:T(8,128)(2,1)S(1)}, u32[]{:S(2)}, u32[]{:S(2)}) collective-permute-start(bf16[1,128,512]{2,1,0:T(8,128)(2,1)S(1)} %get-tuple-element.61), channel_id=1, source_target_pairs={{0,1},{1,2},{2,3},{3,4},{4,5},{5,6},{6,7},{7,8},{8,9},{9,10},{10,1... | collective-permute-start | bytes 393224 | tf_op jit(solution)/shard_map/ppermute | solution.py:17
  156.0 7.2 %collective-permute-start.11 = (bf16[1,128,512]{2,1,0:T(8,128)(2,1)S(1)}, bf16[1,128,512]{2,1,0:T(8,128)(2,1)S(1)}, u32[]{:S(2)}, u32[]{:S(2)}) collective-permute-start(bf16[1,128,512]{2,1,0:T(8,128)(2,1)S(1)} %get-tuple-element.62), channel_id=1, source_target_pairs={{1,0},{2,1},{3,2},{4,3},{5,4},{6,5},{7,6},{8,7},{9,8},{10,9},{11,1... | collective-permute-start | bytes 393224 | tf_op jit(solution)/shard_map/ppermute | solution.py:19
